TPU v7x, 512 devices: a whole 4x4x16 slice. The times are simulated.
512 devices in a mesh: space: 32 (over y, z_lo), chan: 16 (over x, z_hi, core).
Axes of the slice: x: 4, y: 4, z: 16 (z_hi: 2, z_lo: 8; z = z_hi * 8 + z_lo), core: 2. Of those that a mesh axis runs over, the one named last changes fastest.
Arguments:
- latent: bfloat16 [1, 32, 160, 512], P(None, 'space', None, 'chan'), may hold values from -12 to 12
- cache_mid: bfloat16 [2, 32, 160, 512], P(None, 'space', None, 'chan'), may hold values from -6 to 6
- norm1_gain: float32 [512], P('chan'), may hold values from 0.1 to 1.9
- norm1_bias: float32 [512], P('chan'), may hold values from -3 to 3
- conv1_weight: bfloat16 [3, 3, 3, 512, 512], P(None, None, None, 'chan'), may hold values from -0.0625 to 0.0625
- conv1_bias: float32 [512], P('chan'), may hold values from -2 to 2
- cache_up: bfloat16 [2, 64, 320, 512], P(None, 'space', 'chan'), may hold values from -6 to 6
- norm2_gain: float32 [512], replicated, may hold values from 0.1 to 1.9
- norm2_bias: float32 [512], replicated, may hold values from -3 to 3
- conv2_weight: bfloat16 [3, 3, 3, 512, 512], P(None, None, None, None, 'chan'), may hold values from -0.0546875 to 0.0546875
- conv2_bias: float32 [512], replicated, may hold values from -2 to 2
Outputs:
- up_features: bfloat16 [1, 64, 320, 512], P(None, 'space', 'chan')
All inputs are finite; a program needn't handle non-finite values.
Results may differ from a plain program's by a relative error of at most 0.0038.
The roundings to bfloat16 on the way count: a program that leaves them out, or rounds other values in their place, can miss the bound.
Values may be sent and summed in bfloat16 or wider, within the bound.
No kernel may reach another device: no remote copies, remote signals or barrier semaphores. Data moves between devices by JAX's collectives and lax.ppermute only.
A program may use at most 64 MiB of HBM per device.

v0:
```python
import jax
import jax.numpy as jnp
from jax import lax
from jax.sharding import PartitionSpec as P

GROUPS = 32
GS = 16
epsilon = 1e-06


def extended(cells, sides, width):
    for axis, dim in sides:
        count = lax.axis_size(axis)
        ends = count - 1
        head = lax.slice_in_dim(cells, 0, width, axis=dim)
        tail = lax.slice_in_dim(cells, cells.shape[dim] - width, cells.shape[dim], axis=dim)
        cells = jnp.concatenate(
            [
                lax.ppermute(tail, axis, [(i, (i + 1) % count) for i in range(ends)]),
                cells,
                lax.ppermute(head, axis, [((i + 1) % count, i) for i in range(ends)]),
            ],
            axis=dim,
        )
    return cells


def unfold(padded, frames, height, breadth):
    pieces = []
    for shift_time in range(3):
        for shift_row in range(3):
            for shift_col in range(3):
                pieces.append(
                    padded[
                        shift_time : shift_time + frames,
                        shift_row : shift_row + height,
                        shift_col : shift_col + breadth,
                        :,
                    ]
                )
    return jnp.concatenate(pieces, axis=-1)


def norm_apply(upsampled, mean_chan, scale_chan, gain, bias):
    scaled = (upsampled.astype(jnp.float32) - mean_chan) * scale_chan
    return jax.nn.silu(scaled * gain + bias).astype(jnp.bfloat16)


def on_device(
    latent,
    cache_mid,
    norm1_gain,
    norm1_bias,
    conv1_weight,
    conv1_bias,
    cache_up,
    norm2_gain,
    norm2_bias,
    conv2_weight,
    conv2_bias,
):
    frames, height, breadth, chan_here = latent.shape
    groups_here = chan_here // GS
    values = latent.astype(jnp.float32)
    grouped = values.reshape(frames, height, breadth, groups_here, GS)
    entries = frames * height * lax.axis_size("space") * breadth * GS
    group_mean = lax.psum(jnp.sum(grouped, axis=(0, 1, 2, 4)), "space") / entries
    centred = grouped - group_mean[:, None]
    group_var = lax.psum(jnp.sum(centred * centred, axis=(0, 1, 2, 4)), "space") / entries
    scaled = (centred * lax.rsqrt(group_var + epsilon)[:, None]).reshape(
        frames, height, breadth, chan_here
    )
    normed_mid = jax.nn.silu(scaled * norm1_gain + norm1_bias).astype(jnp.bfloat16)
    joined = jnp.concatenate([cache_mid, normed_mid], axis=0)
    rimmed = extended(joined, (("space", 1),), 1)
    padded = jnp.pad(rimmed, ((0, 0), (0, 0), (1, 1), (0, 0)))
    columns = unfold(padded, frames, height, breadth).reshape(frames * height * breadth, -1)
    kernel = conv1_weight.reshape(-1, conv1_weight.shape[-1])
    summed = lax.psum_scatter(
        lax.dot_general(
            kernel, columns, (((0,), (1,)), ((), ())), preferred_element_type=jnp.float32
        ),
        "chan",
        scatter_dimension=0,
        tiled=True,
    )
    conv_mid = summed.T.reshape(frames, height, breadth, chan_here)
    merged = (values + conv_mid + conv1_bias).astype(jnp.bfloat16)
    merged_groups = merged.astype(jnp.float32).reshape(frames, height, breadth, groups_here, GS)
    first_group = lax.axis_index("chan") * groups_here

    def place(partial_value):
        return lax.dynamic_update_slice_in_dim(
            jnp.zeros((GROUPS,), jnp.float32), partial_value, first_group, 0
        )

    own_sum = jnp.sum(merged_groups, axis=(0, 1, 2, 4))
    up_mean = lax.psum(place(own_sum), ("space", "chan")) / entries
    own_mean = lax.dynamic_slice_in_dim(up_mean, first_group, groups_here)
    deviation = merged_groups - own_mean[:, None]
    up_var = (
        lax.psum(place(jnp.sum(deviation * deviation, axis=(0, 1, 2, 4))), ("space", "chan"))
        / entries
    )
    mean_chan = jnp.repeat(up_mean, GS)
    scale_chan = jnp.repeat(lax.rsqrt(up_var + epsilon), GS)
    pixel_tile = lax.all_to_all(merged, "chan", split_axis=2, concat_axis=3, tiled=True)
    upsampled = jnp.repeat(jnp.repeat(pixel_tile, 2, axis=1), 2, axis=2)
    normed_up = norm_apply(upsampled, mean_chan, scale_chan, norm2_gain, norm2_bias)
    joined_up = jnp.concatenate([cache_up, normed_up], axis=0)
    rimmed_up = extended(joined_up, (("space", 1), ("chan", 2)), 1)
    up_height = normed_up.shape[1]
    up_breadth = normed_up.shape[2]
    up_columns = unfold(rimmed_up, frames, up_height, up_breadth).reshape(
        frames * up_height * up_breadth, -1
    )
    kernel_up = conv2_weight.reshape(-1, conv2_weight.shape[-1])
    up_conv = jnp.dot(
        up_columns,
        lax.all_gather(kernel_up, "chan", axis=1, tiled=True),
        preferred_element_type=jnp.float32,
    )
    result = (up_conv + conv2_bias).astype(jnp.bfloat16).reshape(frames, up_height, up_breadth, -1)
    return result


def solution(mesh):
    placed = (
        P(None, "space", None, "chan"),
        P(None, "space", None, "chan"),
        P("chan"),
        P("chan"),
        P(None, None, None, "chan", None),
        P("chan"),
        P(None, "space", "chan", None),
        P(),
        P(),
        P(None, None, None, None, "chan"),
        P(),
    )
    return jax.shard_map(
        on_device,
        mesh=mesh,
        in_specs=placed,
        out_specs=P(None, "space", "chan", None),
        check_vma=False,
    )
```

profile of v0, /device:TPU:480, one launch (start us, length us, event | category | flops | bytes accessed | tf_op | source)
XLA Modules:
  0.0 809.0 jit_solution(2814931638658902125)
XLA Ops:
  6.6 0.9 convert_reduce_fusion
  7.7 103.2 %psum.28 = f32[2]{0:T(128)S(1)} all-reduce(f32[2]{0:T(128)S(1)} %reduce_sum.51), channel_id=1, replica_groups=mesh['space'=32,'chan'=16] {'space'}, use_global_device_ids=true, to_apply=%region_2.0 | all-reduce | flops 2 | bytes 16 | tf_op jit(solution)/shard_map/psum | solution.py:67
  111.0 0.9 fusion.9
  112.1 105.8 %psum.29 = f32[2]{0:T(128)S(1)} all-reduce(f32[2]{0:T(128)S(1)} %reduce_sum.54), channel_id=1, replica_groups=mesh['space'=32,'chan'=16] {'space'}, use_global_device_ids=true, to_apply=%region_5.6 | all-reduce | flops 2 | bytes 16 | tf_op jit(solution)/shard_map/psum | solution.py:69
  218.1 0.8 fusion.17
  219.0 0.8 pad_maximum_fusion.2
  219.7 1.9 collective-permute-start.1
  221.7 11.4 %collective-permute-start = (bf16[3,1,160,32]{2,3,1,0:T(8,128)(2,1)S(1)}, bf16[3,1,160,32]{2,3,1,0:T(8,128)(2,1)S(1)}, u32[]{:S(2)}, u32[]{:S(2)}) collective-permute-start(bf16[3,1,160,32]{2,3,1,0:T(8,128)(2,1)S(1)} %pad_maximum_fusion.2), channel_id=1, source_target_pairs={{0,16},{16,32},{32,48},{48,64},{64,80},{80,96},{96,112},{112,128},... | collective-permute-start | bytes 92168 | tf_op jit(solution)/shard_map/ppermute | solution.py:19
  233.2 2.5 collective-permute-done
  235.7 0.9 select_maximum_fusion
  236.7 0.7 constant_dynamic-update-slice_fusion.22
  237.6 0.7 constant_dynamic-update-slice_fusion.13
  239.3 1.0 copy.154
  240.4 0.8 copy.152
  241.1 2.0 reshape.194
  243.2 106.8 %reduce-scatter.4.cloned.1.call-done = f32[32,160]{1,0:T(8,128)} async-done(((f32[512,160]{1,0:T(8,128)}), f32[32,160]{1,0:T(8,128)}) %reduce-scatter.4.cloned.1.call-update) | async-done | bytes 20496 | tf_op jit(solution)/shard_map/reduce_scatter | solution.py:79
  350.0 0.9 convert_reduce_fusion.1
  351.4 270.6 %psum.30 = f32[32]{0:T(128)S(1)} all-reduce(f32[32]{0:T(128)S(1)} %dynamic_update_slice.6), channel_id=1, replica_groups=mesh['space'=32,'chan'=16] {'space','chan'}, use_global_device_ids=true, to_apply=%region_9.10 | all-reduce | flops 32 | bytes 256 | tf_op jit(solution)/shard_map/psum | solution.py:98
  622.8 100.2 %psum.31 = f32[32]{0:T(128)S(1)} all-reduce(f32[32]{0:T(128)S(1)} %dynamic_update_slice.7), channel_id=1, replica_groups=mesh['space'=32,'chan'=16] {'space','chan'}, use_global_device_ids=true, to_apply=%region_12.13 | all-reduce | flops 32 | bytes 256 | tf_op jit(solution)/shard_map/psum | solution.py:102
  723.6 0.9 reduce.10
  724.5 0.7 reshape.200
  725.2 14.1 %all-to-all-start = ((bf16[16,2,160]{2,1,0:T(2,128)(2,1)}), bf16[16,2,160]{2,1,0:T(2,128)(2,1)S(1)}, u32[]{:S(2)}, u32[]{:S(2)}) async-start(bf16[16,2,160]{2,1,0:T(2,128)(2,1)} %reshape.200), calls=%async_computation | async-start | bytes 32768 | tf_op jit(solution)/shard_map/all_to_all | solution.py:107
  739.7 4.4 all-to-all-done
  744.9 5.9 collective-permute-start.2
  750.8 1.9 collective-permute-start.3
  752.8 1.6 collective-permute-done.2
  754.4 10.8 %collective-permute-done.3 = bf16[3,1,20,512]{3,1,2,0:T(2,128)(2,1)S(1)} collective-permute-done((bf16[3,1,20,512]{3,1,2,0:T(2,128)(2,1)S(1)}, bf16[3,1,20,512]{3,1,2,0:T(2,128)(2,1)S(1)}, u32[]{:S(2)}, u32[]{:S(2)}) %collective-permute-start.3) | collective-permute-done | bytes 61472 | tf_op jit(solution)/shard_map/ppermute | solution.py:21
  765.3 10.6 %collective-permute-start.5 = (bf16[3,4,1,512]{3,1,2,0:T(4,128)(2,1)S(1)}, bf16[3,4,1,512]{3,1,2,0:T(4,128)(2,1)S(1)}, u32[]{:S(2)}, u32[]{:S(2)}) collective-permute-start(bf16[3,4,1,512]{3,1,2,0:T(4,128)(2,1)S(1)} %get-tuple-element.9), channel_id=1, source_target_pairs={{1,0},{2,1},{3,2},{4,3},{5,4},{6,5},{7,6},{8,7},{9,8},{10,9},{11,1... | collective-permute-start | bytes 36872 | tf_op jit(solution)/shard_map/ppermute | solution.py:21
  775.9 1.9 collective-permute-start.4
  778.7 11.0 %collective-permute-done.4 = bf16[3,4,1,512]{3,1,2,0:T(4,128)(2,1)S(1)} collective-permute-done((bf16[3,4,1,512]{3,1,2,0:T(4,128)(2,1)S(1)}, bf16[3,4,1,512]{3,1,2,0:T(4,128)(2,1)S(1)}, u32[]{:S(2)}, u32[]{:S(2)}) %collective-permute-start.4) | collective-permute-done | bytes 12320 | tf_op jit(solution)/shard_map/ppermute | solution.py:19
  789.6 0.7 pad_maximum_fusion
  792.3 9.2 %fusion = bf16[40,512]{1,0:T(8,128)(2,1)S(1)} fusion(bf16[40,13824]{1,0:T(8,128)(2,1)S(1)} %constant_dynamic-update-slice_fusion.27, bf16[13824,512]{0,1:T(8,128)(2,1)} %all-gather.2.cloned.1.call-done, f32[512]{0:T(512)S(1)} %copy-done.6), kind=kOutput, calls=%fused_computation.2 | convolution fusion | flops 566272000 | bytes 15304704 | tf_op jit(solution)/shard_map/dot_general | solution.py:118
  (179 shorter events, 8.0 us)
Async XLA Ops:
  6.5 232.4 %copy-start = (bf16[3,3,3,32,512]{4,3,2,1,0:T(8,128)(2,1)S(1)}, bf16[3,3,3,32,512]{4,3,2,1,0:T(8,128)(2,1)}, u32[]{:S(2)}) copy-start(bf16[3,3,3,32,512]{4,3,2,1,0:T(8,128)(2,1)} %param.15) | copy-start | bytes 2654212
  6.5 232.1 %copy-start.3 = (bf16[1,1,160,32]{2,3,1,0:T(8,128)(2,1)S(1)}, bf16[1,1,160,32]{2,3,1,0:T(8,128)(2,1)}, u32[]{:S(2)}) copy-start(bf16[1,1,160,32]{2,3,1,0:T(8,128)(2,1)} %param.11) | copy-start | bytes 30724
  6.5 232.1 %copy-start.7 = (f32[32]{0:T(128)S(1)}, f32[32]{0:T(128)}, u32[]{:S(2)}) copy-start(f32[32]{0:T(128)} %param.14) | copy-start | bytes 388
  6.5 232.1 %copy-start.8 = (f32[32]{0:T(128)S(1)}, f32[32]{0:T(128)}, u32[]{:S(2)}) copy-start(f32[32]{0:T(128)} %param.13) | copy-start | bytes 388
  6.5 343.4 %reduce-scatter.4.cloned.1.call-start = ((), (), s32[]{:S(2)}) async-start(), calls=%async_computation.3 | async-start | bytes 557056 | tf_op jit(solution)/shard_map/reduce_scatter | solution.py:79
  219.7 13.5 %collective-permute-start.1 = (bf16[3,1,160,32]{2,3,1,0:T(8,128)(2,1)S(1)}, bf16[3,1,160,32]{2,3,1,0:T(8,128)(2,1)S(1)}, u32[]{:S(2)}, u32[]{:S(2)}) collective-permute-start(bf16[3,1,160,32]{2,3,1,0:T(8,128)(2,1)S(1)} %pad_maximum_fusion.2), channel_id=1, source_target_pairs={{16,0},{32,16},{48,32},{64,48},{80,64},{96,80},{112,96},{128,112},... | collective-permute-start | bytes 92168 | tf_op jit(solution)/shard_map/ppermute | solution.py:21
  221.7 14.0 %collective-permute-start = (bf16[3,1,160,32]{2,3,1,0:T(8,128)(2,1)S(1)}, bf16[3,1,160,32]{2,3,1,0:T(8,128)(2,1)S(1)}, u32[]{:S(2)}, u32[]{:S(2)}) collective-permute-start(bf16[3,1,160,32]{2,3,1,0:T(8,128)(2,1)S(1)} %pad_maximum_fusion.2), channel_id=1, source_target_pairs={{0,16},{16,32},{32,48},{48,64},{64,80},{80,96},{96,112},{112,128},... | collective-permute-start | bytes 92168 | tf_op jit(solution)/shard_map/ppermute | solution.py:19
  238.9 1.5 copy-start.2
  240.3 551.7 %all-gather.2.cloned.1.call-start = ((), (), s32[]{:S(2)}) async-start(), calls=%async_computation.2 | async-start | bytes 15040512 | tf_op jit(solution)/shard_map/all_gather | solution.py:120
  241.1 108.9 %copy-start.9 = (f32[32]{0:T(128)S(1)}, f32[32]{0:T(128)}, u32[]{:S(2)}) copy-start(f32[32]{0:T(128)} %param.16) | copy-start | bytes 388
  243.2 501.3 %copy-start.4 = (f32[512]{0:T(512)S(1)}, f32[512]{0:T(512)}, u32[]{:S(2)}) copy-start(f32[512]{0:T(512)} %param.19) | copy-start | bytes 6148
  243.2 501.3 %copy-start.5 = (f32[512]{0:T(512)S(1)}, f32[512]{0:T(512)}, u32[]{:S(2)}) copy-start(f32[512]{0:T(512)} %param.18) | copy-start | bytes 6148
  243.2 501.5 %copy-start.1 = (bf16[2,2,20,512]{3,1,2,0:T(2,128)(2,1)S(1)}, bf16[2,2,20,512]{3,1,2,0:T(2,128)(2,1)}, u32[]{:S(2)}) copy-start(bf16[2,2,20,512]{3,1,2,0:T(2,128)(2,1)} %param.17) | copy-start | bytes 245764
  243.2 509.5 %slice-start = ((bf16[2,2,20,512]{3,1,2,0:T(2,128)(2,1)}), bf16[1,2,20,512]{3,1,2,0:T(2,128)(2,1)S(1)}, s32[]{:S(2)}) async-start(bf16[2,2,20,512]{3,1,2,0:T(2,128)(2,1)} %param.17), calls=%async_computation.4 | async-start | bytes 81920 | tf_op jit(solution)/shard_map/slice | solution.py:34
  725.2 18.9 %all-to-all-start = ((bf16[16,2,160]{2,1,0:T(2,128)(2,1)}), bf16[16,2,160]{2,1,0:T(2,128)(2,1)S(1)}, u32[]{:S(2)}, u32[]{:S(2)}) async-start(bf16[16,2,160]{2,1,0:T(2,128)(2,1)} %reshape.200), calls=%async_computation | async-start | bytes 32768 | tf_op jit(solution)/shard_map/all_to_all | solution.py:107
  744.9 9.5 %collective-permute-start.2 = (bf16[3,1,20,512]{3,1,2,0:T(2,128)(2,1)S(1)}, bf16[3,1,20,512]{3,1,2,0:T(2,128)(2,1)S(1)}, u32[]{:S(2)}, u32[]{:S(2)}) collective-permute-start(bf16[3,1,20,512]{3,1,2,0:T(2,128)(2,1)S(1)} %get-tuple-element.38), channel_id=1, source_target_pairs={{0,16},{16,32},{32,48},{48,64},{64,80},{80,96},{96,112},{112,128},... | collective-permute-start | bytes 184328 | tf_op jit(solution)/shard_map/ppermute | solution.py:19
  750.8 14.5 %collective-permute-start.3 = (bf16[3,1,20,512]{3,1,2,0:T(2,128)(2,1)S(1)}, bf16[3,1,20,512]{3,1,2,0:T(2,128)(2,1)S(1)}, u32[]{:S(2)}, u32[]{:S(2)}) collective-permute-start(bf16[3,1,20,512]{3,1,2,0:T(2,128)(2,1)S(1)} %get-tuple-element.39), channel_id=1, source_target_pairs={{16,0},{32,16},{48,32},{64,48},{80,64},{96,80},{112,96},{128,112},... | collective-permute-start | bytes 184328 | tf_op jit(solution)/shard_map/ppermute | solution.py:21
  765.3 13.4 %collective-permute-start.5 = (bf16[3,4,1,512]{3,1,2,0:T(4,128)(2,1)S(1)}, bf16[3,4,1,512]{3,1,2,0:T(4,128)(2,1)S(1)}, u32[]{:S(2)}, u32[]{:S(2)}) collective-permute-start(bf16[3,4,1,512]{3,1,2,0:T(4,128)(2,1)S(1)} %get-tuple-element.9), channel_id=1, source_target_pairs={{1,0},{2,1},{3,2},{4,3},{5,4},{6,5},{7,6},{8,7},{9,8},{10,9},{11,1... | collective-permute-start | bytes 36872 | tf_op jit(solution)/shard_map/ppermute | solution.py:21
  775.9 13.7 %collective-permute-start.4 = (bf16[3,4,1,512]{3,1,2,0:T(4,128)(2,1)S(1)}, bf16[3,4,1,512]{3,1,2,0:T(4,128)(2,1)S(1)}, u32[]{:S(2)}, u32[]{:S(2)}) collective-permute-start(bf16[3,4,1,512]{3,1,2,0:T(4,128)(2,1)S(1)} %get-tuple-element.10), channel_id=1, source_target_pairs={{0,1},{1,2},{2,3},{3,4},{4,5},{5,6},{6,7},{7,8},{8,9},{9,10},{10,1... | collective-permute-start | bytes 36872 | tf_op jit(solution)/shard_map/ppermute | solution.py:19
  791.6 0.7 copy-start.6
Sparse Core Ops, SparseCore 0:
  240.4 109.5 reduce-scatter.3
  353.3 250.6 all-gather.1
where the time goes:
time: 810 us; the launch traced here: 809 us
  blocking collectives  580 us (72%)
  waiting for transfers between devices  137 us (17%)
  starting transfers between devices  47.9 us (6%)
  between operations  14.4 us (2%)
  local copies, waits for them, and re-layouts  11.5 us (1%)
  matrix products  9.58 us (1%)
  other arithmetic  8.67 us (1%)
    psum x1, blocking collectives, on_device(): up_mean = lax.psum(place(own_sum), ('space', 'chan')) / entries  271 us
    reduce_scatter x1, waiting for transfers between devices, on_device(): lax.psum_scatter(lax.dot_general(kernel, columns, (((0,), (1,)), ((), ())...  107 us
    psum x1, blocking collectives, on_device(): lax.psum(jnp.sum(centred * centred, axis=(0, 1, 2, 4)), 'space') / entries  106 us
    psum x1, blocking collectives, on_device(): lax.psum(jnp.sum(grouped, axis=(0, 1, 2, 4)), 'space') / entries  103 us
    psum x1, blocking collectives, on_device(): lax.psum(place(jnp.sum(deviation * deviation, axis=(0, 1, 2, 4))), ('spac...  100 us
    ppermute x3, starting transfers between devices, extended(): lax.ppermute(tail, axis, [(i, (i + 1) % count) for i in range(ends)])  19.2 us
  transfers between devices with their start and end apart: 9, of which 7 were waited for; matrix products, arithmetic and copies ran while one was open for 1% of the time, Pallas kernels for 0%

commit v1 on v0

--- a/solution.py
+++ b/solution.py
@@ -64,7 +64,9 @@
     values = latent.astype(jnp.float32)
     grouped = values.reshape(frames, height, breadth, groups_here, GS)
     entries = frames * height * lax.axis_size("space") * breadth * GS
-    group_mean = lax.psum(jnp.sum(grouped, axis=(0, 1, 2, 4)), "space") / entries
+    group_mean = (
+        jnp.sum(lax.all_gather(jnp.sum(grouped, axis=(0, 1, 2, 4)), "space"), axis=0) / entries
+    )
     centred = grouped - group_mean[:, None]
     group_var = lax.psum(jnp.sum(centred * centred, axis=(0, 1, 2, 4)), "space") / entries
     scaled = (centred * lax.rsqrt(group_var + epsilon)[:, None]).reshape(

time: 810 us -> 812 us (level)
    psum x1 -> x0, blocking collectives: 103 us -> none  [on_device(): lax.psum(jnp.sum(grouped, axis=(0, 1, 2, 4)), 'space') / entries]
    unnamed x0 -> x1, blocking collectives: none -> 103 us
where the time goes in v1:
time: 812 us; the launch traced here: 811 us
  blocking collectives  580 us (71%)
  waiting for transfers between devices  137 us (17%)
  starting transfers between devices  48 us (6%)
  between operations  15.1 us (2%)
  local copies, waits for them, and re-layouts  13.1 us (2%)
  matrix products  9.59 us (1%)
  other arithmetic  8.7 us (1%)
    psum x1, blocking collectives, on_device(): up_mean = lax.psum(place(own_sum), ('space', 'chan')) / entries  270 us
    reduce_scatter x1, waiting for transfers between devices, on_device(): lax.psum_scatter(lax.dot_general(kernel, columns, (((0,), (1,)), ((), ())...  107 us
    psum x1, blocking collectives, on_device(): lax.psum(jnp.sum(centred * centred, axis=(0, 1, 2, 4)), 'space') / entries  106 us
    unnamed x1, blocking collectives  103 us
    psum x1, blocking collectives, on_device(): lax.psum(place(jnp.sum(deviation * deviation, axis=(0, 1, 2, 4))), ('spac...  100 us
    ppermute x3, starting transfers between devices, extended(): lax.ppermute(tail, axis, [(i, (i + 1) % count) for i in range(ends)])  19.3 us
  transfers between devices with their start and end apart: 9, of which 7 were waited for; matrix products, arithmetic and copies ran while one was open for 1% of the time, Pallas kernels for 0%

profile of v1, /device:TPU:480, one launch (start us, length us, event | category | flops | bytes accessed | tf_op | source)
XLA Modules:
  0.0 811.3 jit_solution(13656464217806238048)
XLA Ops:
  6.6 0.9 convert_reduce_fusion
  7.6 1.3 dynamic-slice
  9.9 103.2 %all-reduce.1 = f32[64]{0:T(128)S(1)} all-reduce(f32[64]{0:T(128)S(1)} %dynamic-update-slice), channel_id=2, replica_groups=mesh['space'=32,'chan'=16] {'space'}, use_global_device_ids=true, to_apply=%add.1 | all-reduce | flops 64 | bytes 512
  113.3 0.9 fusion.9
  114.4 105.8 %psum.21 = f32[2]{0:T(128)S(1)} all-reduce(f32[2]{0:T(128)S(1)} %reduce_sum.66), channel_id=1, replica_groups=mesh['space'=32,'chan'=16] {'space'}, use_global_device_ids=true, to_apply=%region_5.6 | all-reduce | flops 2 | bytes 16 | tf_op jit(solution)/shard_map/psum | solution.py:71
  220.4 0.8 fusion.17
  221.2 0.8 pad_maximum_fusion.2
  222.0 1.9 collective-permute-start.1
  223.9 11.4 %collective-permute-start = (bf16[3,1,160,32]{2,3,1,0:T(8,128)(2,1)S(1)}, bf16[3,1,160,32]{2,3,1,0:T(8,128)(2,1)S(1)}, u32[]{:S(2)}, u32[]{:S(2)}) collective-permute-start(bf16[3,1,160,32]{2,3,1,0:T(8,128)(2,1)S(1)} %pad_maximum_fusion.2), channel_id=1, source_target_pairs={{0,16},{16,32},{32,48},{48,64},{64,80},{80,96},{96,112},{112,128},... | collective-permute-start | bytes 92168 | tf_op jit(solution)/shard_map/ppermute | solution.py:19
  235.5 2.5 collective-permute-done
  238.0 0.9 select_maximum_fusion
  239.0 0.7 constant_dynamic-update-slice_fusion.22
  240.0 0.7 constant_dynamic-update-slice_fusion.13
  241.6 1.0 copy.154
  242.7 0.8 copy.152
  243.5 2.0 reshape.196
  245.5 106.8 %reduce-scatter.4.cloned.1.call-done = f32[32,160]{1,0:T(8,128)} async-done(((f32[512,160]{1,0:T(8,128)}), f32[32,160]{1,0:T(8,128)}) %reduce-scatter.4.cloned.1.call-update) | async-done | bytes 20496 | tf_op jit(solution)/shard_map/reduce_scatter | solution.py:81
  352.3 0.9 convert_reduce_fusion.1
  353.7 270.5 %psum.22 = f32[32]{0:T(128)S(1)} all-reduce(f32[32]{0:T(128)S(1)} %dynamic_update_slice.6), channel_id=1, replica_groups=mesh['space'=32,'chan'=16] {'space','chan'}, use_global_device_ids=true, to_apply=%region_9.10 | all-reduce | flops 32 | bytes 256 | tf_op jit(solution)/shard_map/psum | solution.py:100
  625.1 100.3 %psum.23 = f32[32]{0:T(128)S(1)} all-reduce(f32[32]{0:T(128)S(1)} %dynamic_update_slice.7), channel_id=1, replica_groups=mesh['space'=32,'chan'=16] {'space','chan'}, use_global_device_ids=true, to_apply=%region_12.13 | all-reduce | flops 32 | bytes 256 | tf_op jit(solution)/shard_map/psum | solution.py:104
  726.0 0.9 reduce.10
  727.6 14.1 %all-to-all-start = ((bf16[16,2,160]{2,1,0:T(2,128)(2,1)}), bf16[16,2,160]{2,1,0:T(2,128)(2,1)S(1)}, u32[]{:S(2)}, u32[]{:S(2)}) async-start(bf16[16,2,160]{2,1,0:T(2,128)(2,1)} %reshape.208), calls=%async_computation | async-start | bytes 32768 | tf_op jit(solution)/shard_map/all_to_all | solution.py:109
  742.1 4.4 all-to-all-done
  747.2 5.8 collective-permute-start.2
  753.0 1.9 collective-permute-start.3
  755.1 1.6 collective-permute-done.2
  756.7 10.8 %collective-permute-done.3 = bf16[3,1,20,512]{3,1,2,0:T(2,128)(2,1)S(1)} collective-permute-done((bf16[3,1,20,512]{3,1,2,0:T(2,128)(2,1)S(1)}, bf16[3,1,20,512]{3,1,2,0:T(2,128)(2,1)S(1)}, u32[]{:S(2)}, u32[]{:S(2)}) %collective-permute-start.3) | collective-permute-done | bytes 61472 | tf_op jit(solution)/shard_map/ppermute | solution.py:21
  767.5 10.6 %collective-permute-start.5 = (bf16[3,4,1,512]{3,1,2,0:T(4,128)(2,1)S(1)}, bf16[3,4,1,512]{3,1,2,0:T(4,128)(2,1)S(1)}, u32[]{:S(2)}, u32[]{:S(2)}) collective-permute-start(bf16[3,4,1,512]{3,1,2,0:T(4,128)(2,1)S(1)} %get-tuple-element.9), channel_id=1, source_target_pairs={{1,0},{2,1},{3,2},{4,3},{5,4},{6,5},{7,6},{8,7},{9,8},{10,9},{11,1... | collective-permute-start | bytes 36872 | tf_op jit(solution)/shard_map/ppermute | solution.py:21
  778.2 2.1 collective-permute-start.4
  781.1 10.8 %collective-permute-done.4 = bf16[3,4,1,512]{3,1,2,0:T(4,128)(2,1)S(1)} collective-permute-done((bf16[3,4,1,512]{3,1,2,0:T(4,128)(2,1)S(1)}, bf16[3,4,1,512]{3,1,2,0:T(4,128)(2,1)S(1)}, u32[]{:S(2)}, u32[]{:S(2)}) %collective-permute-start.4) | collective-permute-done | bytes 12320 | tf_op jit(solution)/shard_map/ppermute | solution.py:19
  791.9 0.7 pad_maximum_fusion
  794.5 9.2 %fusion = bf16[40,512]{1,0:T(8,128)(2,1)S(1)} fusion(bf16[40,13824]{1,0:T(8,128)(2,1)S(1)} %constant_dynamic-update-slice_fusion.27, bf16[13824,512]{0,1:T(8,128)(2,1)} %all-gather.3.cloned.1.call-done, f32[512]{0:T(512)S(1)} %copy-done.6), kind=kOutput, calls=%fused_computation.2 | convolution fusion | flops 566272000 | bytes 15304704 | tf_op jit(solution)/shard_map/dot_general | solution.py:120
  (184 shorter events, 9.1 us)
Async XLA Ops:
  6.5 234.7 %copy-start = (bf16[3,3,3,32,512]{4,3,2,1,0:T(8,128)(2,1)S(1)}, bf16[3,3,3,32,512]{4,3,2,1,0:T(8,128)(2,1)}, u32[]{:S(2)}) copy-start(bf16[3,3,3,32,512]{4,3,2,1,0:T(8,128)(2,1)} %param.15) | copy-start | bytes 2654212
  6.5 234.4 %copy-start.3 = (bf16[1,1,160,32]{2,3,1,0:T(8,128)(2,1)S(1)}, bf16[1,1,160,32]{2,3,1,0:T(8,128)(2,1)}, u32[]{:S(2)}) copy-start(bf16[1,1,160,32]{2,3,1,0:T(8,128)(2,1)} %param.11) | copy-start | bytes 30724
  6.5 234.4 %copy-start.7 = (f32[32]{0:T(128)S(1)}, f32[32]{0:T(128)}, u32[]{:S(2)}) copy-start(f32[32]{0:T(128)} %param.14) | copy-start | bytes 388
  6.5 234.4 %copy-start.8 = (f32[32]{0:T(128)S(1)}, f32[32]{0:T(128)}, u32[]{:S(2)}) copy-start(f32[32]{0:T(128)} %param.13) | copy-start | bytes 388
  6.5 345.8 %reduce-scatter.4.cloned.1.call-start = ((), (), s32[]{:S(2)}) async-start(), calls=%async_computation.3 | async-start | bytes 557056 | tf_op jit(solution)/shard_map/reduce_scatter | solution.py:81
  222.0 13.5 %collective-permute-start.1 = (bf16[3,1,160,32]{2,3,1,0:T(8,128)(2,1)S(1)}, bf16[3,1,160,32]{2,3,1,0:T(8,128)(2,1)S(1)}, u32[]{:S(2)}, u32[]{:S(2)}) collective-permute-start(bf16[3,1,160,32]{2,3,1,0:T(8,128)(2,1)S(1)} %pad_maximum_fusion.2), channel_id=1, source_target_pairs={{16,0},{32,16},{48,32},{64,48},{80,64},{96,80},{112,96},{128,112},... | collective-permute-start | bytes 92168 | tf_op jit(solution)/shard_map/ppermute | solution.py:21
  223.9 14.1 %collective-permute-start = (bf16[3,1,160,32]{2,3,1,0:T(8,128)(2,1)S(1)}, bf16[3,1,160,32]{2,3,1,0:T(8,128)(2,1)S(1)}, u32[]{:S(2)}, u32[]{:S(2)}) collective-permute-start(bf16[3,1,160,32]{2,3,1,0:T(8,128)(2,1)S(1)} %pad_maximum_fusion.2), channel_id=1, source_target_pairs={{0,16},{16,32},{32,48},{48,64},{64,80},{80,96},{96,112},{112,128},... | collective-permute-start | bytes 92168 | tf_op jit(solution)/shard_map/ppermute | solution.py:19
  241.2 1.5 copy-start.2
  242.6 551.6 %all-gather.3.cloned.1.call-start = ((), (), s32[]{:S(2)}) async-start(), calls=%async_computation.2 | async-start | bytes 15040512 | tf_op jit(solution)/shard_map/all_gather | solution.py:122
  243.4 108.9 %copy-start.9 = (f32[32]{0:T(128)S(1)}, f32[32]{0:T(128)}, u32[]{:S(2)}) copy-start(f32[32]{0:T(128)} %param.16) | copy-start | bytes 388
  245.5 501.4 %copy-start.4 = (f32[512]{0:T(512)S(1)}, f32[512]{0:T(512)}, u32[]{:S(2)}) copy-start(f32[512]{0:T(512)} %param.19) | copy-start | bytes 6148
  245.5 501.4 %copy-start.5 = (f32[512]{0:T(512)S(1)}, f32[512]{0:T(512)}, u32[]{:S(2)}) copy-start(f32[512]{0:T(512)} %param.18) | copy-start | bytes 6148
  245.5 501.5 %copy-start.1 = (bf16[2,2,20,512]{3,1,2,0:T(2,128)(2,1)S(1)}, bf16[2,2,20,512]{3,1,2,0:T(2,128)(2,1)}, u32[]{:S(2)}) copy-start(bf16[2,2,20,512]{3,1,2,0:T(2,128)(2,1)} %param.17) | copy-start | bytes 245764
  245.5 509.4 %slice-start = ((bf16[2,2,20,512]{3,1,2,0:T(2,128)(2,1)}), bf16[1,2,20,512]{3,1,2,0:T(2,128)(2,1)S(1)}, s32[]{:S(2)}) async-start(bf16[2,2,20,512]{3,1,2,0:T(2,128)(2,1)} %param.17), calls=%async_computation.4 | async-start | bytes 81920 | tf_op jit(solution)/shard_map/slice | solution.py:34
  727.6 18.9 %all-to-all-start = ((bf16[16,2,160]{2,1,0:T(2,128)(2,1)}), bf16[16,2,160]{2,1,0:T(2,128)(2,1)S(1)}, u32[]{:S(2)}, u32[]{:S(2)}) async-start(bf16[16,2,160]{2,1,0:T(2,128)(2,1)} %reshape.208), calls=%async_computation | async-start | bytes 32768 | tf_op jit(solution)/shard_map/all_to_all | solution.py:109
  747.2 9.4 %collective-permute-start.2 = (bf16[3,1,20,512]{3,1,2,0:T(2,128)(2,1)S(1)}, bf16[3,1,20,512]{3,1,2,0:T(2,128)(2,1)S(1)}, u32[]{:S(2)}, u32[]{:S(2)}) collective-permute-start(bf16[3,1,20,512]{3,1,2,0:T(2,128)(2,1)S(1)} %get-tuple-element.38), channel_id=1, source_target_pairs={{0,16},{16,32},{32,48},{48,64},{64,80},{80,96},{96,112},{112,128},... | collective-permute-start | bytes 184328 | tf_op jit(solution)/shard_map/ppermute | solution.py:19
  753.0 14.5 %collective-permute-start.3 = (bf16[3,1,20,512]{3,1,2,0:T(2,128)(2,1)S(1)}, bf16[3,1,20,512]{3,1,2,0:T(2,128)(2,1)S(1)}, u32[]{:S(2)}, u32[]{:S(2)}) collective-permute-start(bf16[3,1,20,512]{3,1,2,0:T(2,128)(2,1)S(1)} %get-tuple-element.39), channel_id=1, source_target_pairs={{16,0},{32,16},{48,32},{64,48},{80,64},{96,80},{112,96},{128,112},... | collective-permute-start | bytes 184328 | tf_op jit(solution)/shard_map/ppermute | solution.py:21
  767.5 13.6 %collective-permute-start.5 = (bf16[3,4,1,512]{3,1,2,0:T(4,128)(2,1)S(1)}, bf16[3,4,1,512]{3,1,2,0:T(4,128)(2,1)S(1)}, u32[]{:S(2)}, u32[]{:S(2)}) collective-permute-start(bf16[3,4,1,512]{3,1,2,0:T(4,128)(2,1)S(1)} %get-tuple-element.9), channel_id=1, source_target_pairs={{1,0},{2,1},{3,2},{4,3},{5,4},{6,5},{7,6},{8,7},{9,8},{10,9},{11,1... | collective-permute-start | bytes 36872 | tf_op jit(solution)/shard_map/ppermute | solution.py:21
  778.2 13.7 %collective-permute-start.4 = (bf16[3,4,1,512]{3,1,2,0:T(4,128)(2,1)S(1)}, bf16[3,4,1,512]{3,1,2,0:T(4,128)(2,1)S(1)}, u32[]{:S(2)}, u32[]{:S(2)}) collective-permute-start(bf16[3,4,1,512]{3,1,2,0:T(4,128)(2,1)S(1)} %get-tuple-element.10), channel_id=1, source_target_pairs={{0,1},{1,2},{2,3},{3,4},{4,5},{5,6},{6,7},{7,8},{8,9},{9,10},{10,1... | collective-permute-start | bytes 36872 | tf_op jit(solution)/shard_map/ppermute | solution.py:19
  793.9 0.7 copy-start.6
Sparse Core Ops, SparseCore 0:
  242.7 109.5 reduce-scatter.3
  355.6 250.0 all-gather.2
